TPU v7x, 128 devices: a whole 4x4x4 slice. The times are simulated.
128 devices in a mesh: section: 2 (over x_lo), expert: 16 (over z, x_hi, core), dp: 4 (over y).
Axes of the slice: x: 4 (x_hi: 2, x_lo: 2; x = x_hi * 2 + x_lo), y: 4, z: 4, core: 2. Of those that a mesh axis runs over, the one named last changes fastest.
Arguments:
- fresh_tokens: bfloat16 [2, 4096, 4096], P(None, ('expert', 'dp')), may hold values from -60 to 60
- in_flight: bfloat16 [4096, 4096], P(('expert', 'dp')), may hold values from -60 to 60
- norm_weight: float32 [2, 4096], P('section'), may hold values from 0.1 to 1.9
- gate_up: bfloat16 [2, 16, 2, 4096, 768], P('section', 'expert', None, 'dp'), may hold values from -0.09375 to 0.09375
- down_proj: bfloat16 [2, 16, 768, 4096], P('section', 'expert', 'dp'), may hold values from -0.21875 to 0.21875
- first_moment: bfloat16 [2, 16, 768, 4096], P('section', 'expert', 'dp'), may hold values from -6 to 6
- second_moment: bfloat16 [2, 16, 768, 4096], P('section', 'expert', 'dp'), may hold values from 0.099609375 to 4
- route_ids: int32 [2, 2, 4096, 8], P('section', None, ('expert', 'dp')), may hold values from 0 to 15, all different within a row; in each aligned block of 64 rows (0 to 63, 64 to 127, ..., all dimensions but the last counted through in order) at most 36 rows name the same one
- route_probs: float32 [2, 2, 4096, 8], P('section', None, ('expert', 'dp')), may hold values from 0.05 to 1
- trade_flags: int32 [8, 1], replicated, may hold values from 0 to 1, as said below
Outputs:
- layer_out: bfloat16 [2, 2, 4096, 4096], P('section', None, ('expert', 'dp'))
- gate_up_moved: bfloat16 [2, 16, 2, 4096, 768], P('section', 'expert', None, 'dp')
- down_moved: bfloat16 [2, 16, 768, 4096], P('section', 'expert', 'dp')
- first_moved: bfloat16 [2, 16, 768, 4096], P('section', 'expert', 'dp')
- second_moved: bfloat16 [2, 16, 768, 4096], P('section', 'expert', 'dp')
Inputs may be any that keep to these rules, and one draw needn't show every extreme that they name: `route_ids`: in each aligned block of 64 rows (one device's tokens of one section and tick) the 8 experts of a token differ and no expert is chosen by more than 36 rows. `trade_flags`: at least one entry is 1 and at least one is 0.
All inputs are finite; a program needn't handle non-finite values.
Results may differ from a plain program's by a relative error of at most 0.0035.
Values may be sent and summed in bfloat16 or wider, within the bound.
A program may use at most 128 MiB of HBM per device.

v0:
```python
import jax
import jax.numpy as jnp
from jax import lax
from jax.sharding import PartitionSpec as P

EXPERTS = 16


def partner(value, axis, bit):
    return lax.ppermute(value, axis, [(i, i ^ 1 << bit) for i in range(lax.axis_size(axis))])


def shifted(block, axis, distance):
    devices = range(lax.axis_size(axis))
    route = [(i - distance, i) for i in devices if i - distance in devices]
    return lax.ppermute(block, axis, route)


def rms_normed(inputs, norm_gain):
    values = inputs.astype(jnp.float32)
    inverse_rms = lax.rsqrt(jnp.mean(values * values, axis=-1, keepdims=True) + 1e-06)
    return (values * inverse_rms * norm_gain).astype(jnp.bfloat16)


def per_device(
    fresh_tokens,
    in_flight,
    norm_weight,
    gate_up,
    down_proj,
    first_moment,
    second_moment,
    route_ids,
    route_probs,
    trade_flags,
):
    groups = lax.axis_size("expert")
    half_span = groups // 2
    top_bit = groups.bit_length() - 2
    own_rank = lax.axis_index("expert")
    section_index = lax.axis_index("section")
    full_gate_up = lax.all_gather(gate_up, "dp", axis=3, tiled=True)
    full_down = lax.all_gather(down_proj, "dp", axis=2, tiled=True)
    gate_weights = full_gate_up[0, 0, 0]
    up_weights = full_gate_up[0, 0, 1]
    down_weights = full_down[0, 0]
    expert_ids = jnp.arange(EXPERTS, dtype=jnp.int32)
    probs = route_probs[0]
    mix = probs / jnp.sum(probs, axis=-1, keepdims=True)
    chosen = route_ids[0][:, :, :, None] == expert_ids
    dense_mix = jnp.sum(jnp.where(chosen, mix[:, :, :, None], 0.0), axis=2)
    all_mix = lax.all_gather(dense_mix, "expert", axis=1, tiled=True)
    own_mix = jnp.sum(jnp.where(expert_ids == own_rank, all_mix, 0.0), axis=-1)
    traded = partner((gate_up, down_proj, first_moment, second_moment), "expert", top_bit)

    def layer(inputs, scale, held=None):
        normed = rms_normed(inputs, norm_weight[0])
        arrived = lax.all_gather(normed, "expert", axis=0, tiled=True)
        gate_part = jnp.dot(arrived, gate_weights, preferred_element_type=jnp.float32)
        up_part = jnp.dot(arrived, up_weights, preferred_element_type=jnp.float32)
        active = (jax.nn.silu(gate_part) * up_part).astype(jnp.bfloat16)
        result = jnp.dot(active, down_weights, preferred_element_type=jnp.float32)
        result = (result * scale[:, None]).astype(jnp.bfloat16)
        if held is not None:
            result, held = lax.optimization_barrier((result, held))
        combined = lax.psum_scatter(result, "expert", scatter_dimension=0, tiled=True)
        return (
            (inputs.astype(jnp.float32) + combined.astype(jnp.float32)).astype(jnp.bfloat16),
            held,
        )

    first_input = jnp.where(section_index == 0, fresh_tokens[0], in_flight)
    tick_zero, traded = layer(first_input, own_mix[0], traded)
    arrived = shifted(tick_zero, "section", 1)
    second_input = jnp.where(section_index == 0, fresh_tokens[1], arrived)
    tick_one, _ = layer(second_input, own_mix[1])
    layer_out = jnp.stack([tick_zero, tick_one])[None]
    own_flags = trade_flags[own_rank % half_span] == 1
    mask_five = own_flags[None, :, None, None, None]
    mask_four = own_flags[None, :, None, None]
    gate_up_moved = jnp.where(mask_five, traded[0], gate_up)
    down_moved = jnp.where(mask_four, traded[1], down_proj)
    first_moved = jnp.where(mask_four, traded[2], first_moment)
    second_moved = jnp.where(mask_four, traded[3], second_moment)
    return (layer_out, gate_up_moved, down_moved, first_moved, second_moved)


def solution(mesh):
    return jax.shard_map(
        per_device,
        mesh=mesh,
        in_specs=(
            P(None, ("expert", "dp"), None),
            P(("expert", "dp"), None),
            P("section", None),
            P("section", "expert", None, "dp", None),
            P("section", "expert", "dp", None),
            P("section", "expert", "dp", None),
            P("section", "expert", "dp", None),
            P("section", None, ("expert", "dp"), None),
            P("section", None, ("expert", "dp"), None),
            P(),
        ),
        out_specs=(
            P("section", None, ("expert", "dp"), None),
            P("section", "expert", None, "dp", None),
            P("section", "expert", "dp", None),
            P("section", "expert", "dp", None),
            P("section", "expert", "dp", None),
        ),
        check_vma=False,
    )
```

profile of v0, /device:TPU:0, one launch (start us, length us, event | category | flops | bytes accessed | tf_op | source)
XLA Modules:
  0.0 780.1 jit_solution(14578231850789856475)
XLA Ops:
  7.2 1.3 fusion.6
  9.4 1.8 fusion.8
  12.8 4.0 collective-permute-start.1
  16.9 3.4 collective-permute-start.2
  20.6 35.1 %all_gather.18 = f32[2,1024,16]{2,0,1:T(2,128)S(1)} all-gather(f32[2,64,16]{2,0,1:T(2,128)S(1)} %copy.17), channel_id=1, replica_groups=mesh['section'=2,'expert'=16,'dp'=4] {'expert'}, dimensions={1}, use_global_device_ids=true | all-gather | bytes 139264 | tf_op jit(solution)/shard_map/all_gather | solution.py:52
  59.2 187.8 %all-gather.5.cloned.1.call-done = bf16[1024,4096]{1,0:T(8,128)(2,1)} async-done(((bf16[64,4096]{1,0:T(8,128)(2,1)}), bf16[1024,4096]{1,0:T(8,128)(2,1)}) %all-gather.5.cloned.1.call-update) | async-done | bytes 8388624 | tf_op jit(solution)/shard_map/all_gather | solution.py:58
  247.0 118.0 %all-gather.7.cloned.1.call-done = bf16[1,1,2,4096,768]{4,3,2,1,0:T(8,128)(2,1)} async-done(((bf16[1,1,2,1024,768]{4,3,2,1,0:T(8,128)(2,1)}), bf16[1,1,2,4096,768]{4,3,2,1,0:T(8,128)(2,1)}) %all-gather.7.cloned.1.call-update) | async-done | bytes 12582928 | tf_op jit(solution)/shard_map/all_gather | solution.py:42
  365.0 11.0 %fusion.5 = f32[1024,768]{1,0:T(8,128)S(1)} fusion(bf16[1024,4096]{1,0:T(8,128)(2,1)} %all-gather.5.cloned.1.call-done, bf16[1,1,2,4096,768]{4,3,2,1,0:T(8,128)(2,1)} %all-gather.7.cloned.1.call-done), kind=kOutput, calls=%fused_computation.9 | convolution fusion | flops 6442450944 | bytes 17825792 | tf_op jit(solution)/shard_map/dot_general | solution.py:60
  376.2 8.1 %multiply_convert_fusion.3 = bf16[1024,768]{1,0:T(8,128)(2,1)} fusion(f32[1024,768]{1,0:T(8,128)S(1)} %fusion.5, bf16[1024,4096]{1,0:T(8,128)(2,1)S(1)} %copy-done.13, bf16[1,1,2,4096,768]{4,3,2,1,0:T(8,128)(2,1)S(1)} %copy-done.12), kind=kOutput, calls=%fused_computation.11 | convolution fusion | flops 6447169536 | bytes 19398656 | tf_op jit(solution)/shard_map/dot_general | solution.py:59
  384.2 49.1 %all-gather.9.cloned.1.call-done = bf16[1,1,768,4096]{3,2,1,0:T(8,128)(2,1)} async-done(((bf16[1,1,192,4096]{3,2,1,0:T(8,128)(2,1)}), bf16[1,1,768,4096]{3,2,1,0:T(8,128)(2,1)}) %all-gather.9.cloned.1.call-update) | async-done | bytes 6291472 | tf_op jit(solution)/shard_map/all_gather | solution.py:43
  433.4 11.2 %multiply_convert_fusion.1 = bf16[1024,4096]{1,0:T(8,128)(2,1)} fusion(f32[1024]{0:T(1024)S(1)} %bitcast.45, bf16[1024,768]{1,0:T(8,128)(2,1)} %multiply_convert_fusion.3, bf16[1,1,768,4096]{3,2,1,0:T(8,128)(2,1)} %all-gather.9.cloned.1.call-done), kind=kOutput, calls=%fused_computation.1 | convolution fusion | flops 6450839552 | bytes 16257024 | tf_op jit(solution)/shard_map/dot_general | solution.py:62
  444.7 103.2 %reduce-scatter.3.cloned.1.call-done = bf16[64,4096]{1,0:T(8,128)(2,1)} async-done(((bf16[1024,4096]{1,0:T(8,128)(2,1)}), bf16[64,4096]{1,0:T(8,128)(2,1)}) %reduce-scatter.3.cloned.1.call-update) | async-done | bytes 524304 | tf_op jit(solution)/shard_map/reduce_scatter | solution.py:66
  547.9 1.3 fusion.9
  549.3 2.5 collective-permute-start.4
  551.8 10.1 %collective-permute-done.4 = bf16[64,4096]{1,0:T(8,128)(2,1)S(1)} collective-permute-done((bf16[64,4096]{1,0:T(8,128)(2,1)S(1)}, bf16[64,4096]{1,0:T(8,128)(2,1)S(1)}, u32[]{:S(2)}, u32[]{:S(2)}) %collective-permute-start.4) | collective-permute-done | bytes 524320 | tf_op jit(solution)/shard_map/ppermute | solution.py:16
  561.9 1.3 fusion.10
  566.5 71.6 %all-gather.11.cloned.1.call-done = bf16[1024,4096]{1,0:T(8,128)(2,1)} async-done(((bf16[64,4096]{1,0:T(8,128)(2,1)}), bf16[1024,4096]{1,0:T(8,128)(2,1)}) %all-gather.11.cloned.1.call-update) | async-done | bytes 8388624 | tf_op jit(solution)/shard_map/all_gather | solution.py:58
  638.1 11.0 %fusion.4 = f32[1024,768]{1,0:T(8,128)S(1)} fusion(bf16[1024,4096]{1,0:T(8,128)(2,1)} %all-gather.11.cloned.1.call-done, bf16[1,1,2,4096,768]{4,3,2,1,0:T(8,128)(2,1)} %all-gather.7.cloned.1.call-done), kind=kOutput, calls=%fused_computation.8 | convolution fusion | flops 6442450944 | bytes 17825792 | tf_op jit(solution)/shard_map/dot_general | solution.py:60
  649.1 9.8 %multiply_convert_fusion.2 = bf16[1024,768]{1,0:T(8,128)(2,1)S(1)} fusion(f32[1024,768]{1,0:T(8,128)S(1)} %fusion.4, bf16[1024,4096]{1,0:T(8,128)(2,1)S(1)} %copy-done.14, bf16[1,1,2,4096,768]{4,3,2,1,0:T(8,128)(2,1)} %all-gather.7.cloned.1.call-done), kind=kOutput, calls=%fused_computation.10 | convolution fusion | flops 6447169536 | bytes 19398656 | tf_op jit(solution)/shard_map/dot_general | solution.py:59
  658.9 11.7 %multiply_convert_fusion = bf16[1024,4096]{1,0:T(8,128)(2,1)} fusion(f32[1024]{0:T(1024)S(1)} %bitcast.46, bf16[1024,768]{1,0:T(8,128)(2,1)S(1)} %multiply_convert_fusion.2, bf16[1,1,768,4096]{3,2,1,0:T(8,128)(2,1)} %all-gather.9.cloned.1.call-done), kind=kOutput, calls=%fused_computation | convolution fusion | flops 6450839552 | bytes 16257024 | tf_op jit(solution)/shard_map/dot_general | solution.py:62
  671.9 4.6 broadcast_select_fusion
  676.6 4.0 broadcast_select_fusion.3
  680.5 4.9 broadcast_select_fusion.1
  685.4 85.6 %reduce-scatter.5.cloned.1.call-done = bf16[64,4096]{1,0:T(8,128)(2,1)} async-done(((bf16[1024,4096]{1,0:T(8,128)(2,1)}), bf16[64,4096]{1,0:T(8,128)(2,1)}) %reduce-scatter.5.cloned.1.call-update) | async-done | bytes 524304 | tf_op jit(solution)/shard_map/reduce_scatter | solution.py:66
  (65 shorter events, 13.2 us)
Async XLA Ops:
  7.2 239.8 %all-gather.5.cloned.1.call-start = ((), (), s32[]{:S(2)}) async-start(), calls=%async_computation.2 | async-start | bytes 8912896 | tf_op jit(solution)/shard_map/all_gather | solution.py:58
  9.4 7.5 copy-start
  9.4 11.1 %copy-start.10 = (f32[1,2,64,8]{2,3,1,0:T(8,128)S(1)}, f32[1,2,64,8]{2,3,1,0:T(8,128)}, u32[]{:S(2)}) copy-start(f32[1,2,64,8]{2,3,1,0:T(8,128)} %param.18) | copy-start | bytes 12292
  9.4 11.1 %copy-start.11 = (s32[1,2,64,8]{2,3,1,0:T(8,128)S(1)}, s32[1,2,64,8]{2,3,1,0:T(8,128)}, u32[]{:S(2)}) copy-start(s32[1,2,64,8]{2,3,1,0:T(8,128)} %param.17) | copy-start | bytes 12292
  11.2 353.7 %all-gather.7.cloned.1.call-start = ((), (), s32[]{:S(2)}) async-start(), calls=%async_computation.3 | async-start | bytes 15728640 | tf_op jit(solution)/shard_map/all_gather | solution.py:42
  12.0 421.4 %all-gather.9.cloned.1.call-start = ((), (), s32[]{:S(2)}) async-start(), calls=%async_computation.4 | async-start | bytes 7864320 | tf_op jit(solution)/shard_map/all_gather | solution.py:43
  12.7 535.2 %reduce-scatter.3.cloned.1.call-start = ((), (), s32[]{:S(2)}) async-start(), calls=%async_computation.5 | async-start | bytes 8912896 | tf_op jit(solution)/shard_map/reduce_scatter | solution.py:66
  12.8 431.9 %collective-permute-start.1 = (bf16[1,1,192,4096]{3,2,1,0:T(8,128)(2,1)}, bf16[1,1,192,4096]{3,2,1,0:T(8,128)(2,1)}, u32[]{:S(2)}, u32[]{:S(2)}) collective-permute-start(bf16[1,1,192,4096]{3,2,1,0:T(8,128)(2,1)} %param.14), channel_id=1, source_target_pairs={{0,32},{4,36},{8,40},{12,44},{16,48},{20,52},{24,56},{28,60},{32,0... | collective-permute-start | bytes 4718600 | tf_op jit(solution)/shard_map/ppermute | solution.py:10
  16.8 427.8 %collective-permute-start = (bf16[1,1,2,1024,768]{4,3,2,1,0:T(8,128)(2,1)S(1)}, bf16[1,1,2,1024,768]{4,3,2,1,0:T(8,128)(2,1)}, u32[]{:S(2)}, u32[]{:S(2)}) collective-permute-start(bf16[1,1,2,1024,768]{4,3,2,1,0:T(8,128)(2,1)S(1)} %copy-done), channel_id=1, source_target_pairs={{0,32},{4,36},{8,40},{12,44},{16,48},{20,52},{24,56},{28,60},{32,0... | collective-permute-start | bytes 9437192 | tf_op jit(solution)/shard_map/ppermute | solution.py:10
  16.9 427.7 %collective-permute-start.2 = (bf16[1,1,192,4096]{3,2,1,0:T(8,128)(2,1)}, bf16[1,1,192,4096]{3,2,1,0:T(8,128)(2,1)}, u32[]{:S(2)}, u32[]{:S(2)}) collective-permute-start(bf16[1,1,192,4096]{3,2,1,0:T(8,128)(2,1)} %param.15), channel_id=1, source_target_pairs={{0,32},{4,36},{8,40},{12,44},{16,48},{20,52},{24,56},{28,60},{32,0... | collective-permute-start | bytes 4718600 | tf_op jit(solution)/shard_map/ppermute | solution.py:10
  20.3 424.3 %collective-permute-start.3 = (bf16[1,1,192,4096]{3,2,1,0:T(8,128)(2,1)}, bf16[1,1,192,4096]{3,2,1,0:T(8,128)(2,1)}, u32[]{:S(2)}, u32[]{:S(2)}) collective-permute-start(bf16[1,1,192,4096]{3,2,1,0:T(8,128)(2,1)} %param.16), channel_id=1, source_target_pairs={{0,32},{4,36},{8,40},{12,44},{16,48},{20,52},{24,56},{28,60},{32,0... | collective-permute-start | bytes 4718600 | tf_op jit(solution)/shard_map/ppermute | solution.py:10
  365.0 11.0 %copy-start.12 = (bf16[1,1,2,4096,768]{4,3,2,1,0:T(8,128)(2,1)S(1)}, bf16[1,1,2,4096,768]{4,3,2,1,0:T(8,128)(2,1)}, u32[]{:S(2)}) copy-start(bf16[1,1,2,4096,768]{4,3,2,1,0:T(8,128)(2,1)} %all-gather.7.cloned.1.call-done) | copy-start | bytes 37748740
  365.0 11.2 %copy-start.13 = (bf16[1024,4096]{1,0:T(8,128)(2,1)S(1)}, bf16[1024,4096]{1,0:T(8,128)(2,1)}, u32[]{:S(2)}) copy-start(bf16[1024,4096]{1,0:T(8,128)(2,1)} %all-gather.5.cloned.1.call-done) | copy-start | bytes 25165828
  444.7 119.3 %copy-start.9 = (f32[1,4096]{1,0:T(1,128)S(1)}, f32[1,4096]{1,0:T(1,128)}, u32[]{:S(2)}) copy-start(f32[1,4096]{1,0:T(1,128)} %param.12) | copy-start | bytes 49156
  444.7 193.4 %all-gather.11.cloned.1.call-start = ((), (), s32[]{:S(2)}) async-start(), calls=%async_computation.6 | async-start | bytes 8912896 | tf_op jit(solution)/shard_map/all_gather | solution.py:58
  549.3 2.5 copy-start.5
  549.3 12.6 %collective-permute-start.4 = (bf16[64,4096]{1,0:T(8,128)(2,1)S(1)}, bf16[64,4096]{1,0:T(8,128)(2,1)S(1)}, u32[]{:S(2)}, u32[]{:S(2)}) collective-permute-start(bf16[64,4096]{1,0:T(8,128)(2,1)S(1)} %fusion.9), channel_id=1, source_target_pairs={{0,64},{1,65},{2,66},{3,67},{4,68},{5,69},{6,70},{7,71},{8,72},{9,... | collective-permute-start | bytes 1572872 | tf_op jit(solution)/shard_map/ppermute | solution.py:16
  565.0 206.0 %reduce-scatter.5.cloned.1.call-start = ((), (), s32[]{:S(2)}) async-start(), calls=%async_computation.7 | async-start | bytes 8912896 | tf_op jit(solution)/shard_map/reduce_scatter | solution.py:66
  638.1 11.1 %copy-start.14 = (bf16[1024,4096]{1,0:T(8,128)(2,1)S(1)}, bf16[1024,4096]{1,0:T(8,128)(2,1)}, u32[]{:S(2)}) copy-start(bf16[1024,4096]{1,0:T(8,128)(2,1)} %all-gather.11.cloned.1.call-done) | copy-start | bytes 25165828
  671.9 4.7 copy-start.1
  676.6 4.0 copy-start.7
  676.6 4.0 copy-start.8
  680.5 90.5 %copy-start.4 = (bf16[64,4096]{1,0:T(8,128)(2,1)S(1)}, bf16[64,4096]{1,0:T(8,128)(2,1)}, u32[]{:S(2)}) copy-start(bf16[64,4096]{1,0:T(8,128)(2,1)} %copy-done.3) | copy-start | bytes 1572868
  680.5 91.6 %copy-start.6 = (bf16[64,4096]{1,0:T(8,128)(2,1)S(1)}, bf16[64,4096]{1,0:T(8,128)(2,1)}, u32[]{:S(2)}) copy-start(bf16[64,4096]{1,0:T(8,128)(2,1)} %copy-done.5) | copy-start | bytes 1572868
  (3 other events, 2.3 us)
Sparse Core Ops, SparseCore 0:
  11.4 235.5 all-gather.4
  248.6 116.2 all-gather.6
  366.6 66.6 all-gather.8
  444.8 103.1 reduce-scatter.2
  565.1 72.8 all-gather.10
  670.8 100.1 reduce-scatter.4
where the time goes:
time: 781 us; the launch traced here: 780 us
  waiting for transfers between devices  627 us (80%)
  matrix products  62.9 us (8%)
  blocking collectives  35.1 us (4%)
  other arithmetic  24.4 us (3%)
  between operations  14.3 us (2%)
  starting transfers between devices  10.6 us (1%)
    all_gather x2, waiting for transfers between devices, layer(): arrived = lax.all_gather(normed, 'expert', axis=0, tiled=True)  259 us
    reduce_scatter x2, waiting for transfers between devices, layer(): lax.psum_scatter(result, 'expert', scatter_dimension=0, tiled=True)  189 us
    all_gather x1, waiting for transfers between devices, per_device(): full_gate_up = lax.all_gather(gate_up, 'dp', axis=3, tiled=True)  118 us
    all_gather x1, waiting for transfers between devices, per_device(): full_down = lax.all_gather(down_proj, 'dp', axis=2, tiled=True)  49.1 us
    all_gather x1, blocking collectives, per_device(): all_mix = lax.all_gather(dense_mix, 'expert', axis=1, tiled=True)  35.1 us
    dot_general x2, matrix products, layer(): result = jnp.dot(active, down_weights, preferred_element_type=jnp.float32)  23 us
    dot_general x2, matrix products, layer(): up_part = jnp.dot(arrived, up_weights, preferred_element_type=jnp.float32)  22.1 us
    dot_general x2, matrix products, layer(): jnp.dot(arrived, gate_weights, preferred_element_type=jnp.float32)  17.8 us
  transfers between devices with their start and end apart: 11, of which 7 were waited for; matrix products, arithmetic and copies ran while one was open for 6% of the time, Pallas kernels for 0%

commit v1 on v0

--- a/solution.py
+++ b/solution.py
@@ -40,7 +40,12 @@
     own_rank = lax.axis_index("expert")
     section_index = lax.axis_index("section")
     full_gate_up = lax.all_gather(gate_up, "dp", axis=3, tiled=True)
-    full_down = lax.all_gather(down_proj, "dp", axis=2, tiled=True)
+    ring = [down_proj]
+    for hop in range(3):
+        ring.append(lax.ppermute(ring[-1], "dp", [(dev, (dev + 1) % 4) for dev in range(4)]))
+    full_down = jnp.roll(
+        jnp.concatenate(ring[::-1], axis=2), (lax.axis_index("dp") + 1) * ring[0].shape[2], axis=2
+    )
     gate_weights = full_gate_up[0, 0, 0]
     up_weights = full_gate_up[0, 0, 1]
     down_weights = full_down[0, 0]

time: 781 us -> 600 us (0.77)
  waiting for transfers between devices: 627 us -> 434 us
  local copies, waits for them, and re-layouts: 6.06 us -> 20.3 us
    all_gather x2, waiting for transfers between devices: 259 us -> 72.7 us  [layer(): arrived = lax.all_gather(normed, 'expert', axis=0, tiled=True)]
    ppermute x0 -> x3, waiting for transfers between devices: none -> 87.1 us  [per_device(): lax.ppermute(ring[-1], 'dp', [(dev, (dev + 1) % 4) for dev in range(4)])]
    all_gather x1, waiting for transfers between devices: 118 us -> 63.3 us  [per_device(): full_gate_up = lax.all_gather(gate_up, 'dp', axis=3, tiled=True)]
    all_gather x1 -> x0, waiting for transfers between devices: 49.1 us -> none  [per_device(): full_down = lax.all_gather(down_proj, 'dp', axis=2, tiled=True)]
    unnamed x34 -> x35, local copies, waits for them, and re-layouts: 4.86 us -> 17.7 us
    ppermute x4, waiting for transfers between devices: 0.01 us -> 12 us  [partner(): lax.ppermute(value, axis, [(i, i ^ 1 << bit) for i in range(lax.axis_size...]
  transfers between devices with their start and end apart: 11 -> 13, of which waited for: 7 -> 9; matrix products, arithmetic and copies ran while one was open for 6% -> 11% of each run, Pallas kernels for 0% -> 0%
where the time goes in v1:
time: 600 us; the launch traced here: 599 us
  waiting for transfers between devices  434 us (72%)
  matrix products  62.6 us (10%)
  blocking collectives  32.1 us (5%)
  other arithmetic  24 us (4%)
  local copies, waits for them, and re-layouts  20.3 us (3%)
  between operations  14 us (2%)
  starting transfers between devices  12.1 us (2%)
    reduce_scatter x2, waiting for transfers between devices, layer(): lax.psum_scatter(result, 'expert', scatter_dimension=0, tiled=True)  188 us
    ppermute x3, waiting for transfers between devices, per_device(): lax.ppermute(ring[-1], 'dp', [(dev, (dev + 1) % 4) for dev in range(4)])  87.1 us
    all_gather x2, waiting for transfers between devices, layer(): arrived = lax.all_gather(normed, 'expert', axis=0, tiled=True)  72.7 us
    all_gather x1, waiting for transfers between devices, per_device(): full_gate_up = lax.all_gather(gate_up, 'dp', axis=3, tiled=True)  63.3 us
    all_gather x1, blocking collectives, per_device(): all_mix = lax.all_gather(dense_mix, 'expert', axis=1, tiled=True)  32.1 us
    dot_general x2, matrix products, layer(): result = jnp.dot(active, down_weights, preferred_element_type=jnp.float32)  23.7 us
    dot_general x2, matrix products, layer(): up_part = jnp.dot(arrived, up_weights, preferred_element_type=jnp.float32)  22.1 us
    unnamed x35, local copies, waits for them, and re-layouts  17.7 us
  transfers between devices with their start and end apart: 13, of which 9 were waited for; matrix products, arithmetic and copies ran while one was open for 11% of the time, Pallas kernels for 0%

profile of v1, /device:TPU:0, one launch (start us, length us, event | category | flops | bytes accessed | tf_op | source)
XLA Modules:
  0.0 599.3 jit_solution(512642681661372742)
XLA Ops:
  13.8 35.8 %collective-permute-done = bf16[1,1,192,4096]{3,2,1,0:T(8,128)(2,1)S(1)} collective-permute-done((bf16[1,1,192,4096]{3,2,1,0:T(8,128)(2,1)S(1)}, bf16[1,1,192,4096]{3,2,1,0:T(8,128)(2,1)S(1)}, u32[]{:S(2)}, u32[]{:S(2)}) %collective-permute-start) | collective-permute-done | bytes 1572896 | tf_op jit(solution)/shard_map/ppermute | solution.py:45
  49.9 36.4 %collective-permute-done.1 = bf16[1,1,192,4096]{3,2,1,0:T(8,128)(2,1)} collective-permute-done((bf16[1,1,192,4096]{3,2,1,0:T(8,128)(2,1)S(1)}, bf16[1,1,192,4096]{3,2,1,0:T(8,128)(2,1)}, u32[]{:S(2)}, u32[]{:S(2)}) %collective-permute-start.1) | collective-permute-done | bytes 1572896 | tf_op jit(solution)/shard_map/ppermute | solution.py:45
  86.3 3.8 collective-permute-start.3
  90.2 3.5 collective-permute-start.5
  93.9 32.1 %all_gather.14 = f32[2,1024,16]{2,0,1:T(2,128)S(1)} all-gather(f32[2,64,16]{2,0,1:T(2,128)S(1)} %copy.17), channel_id=1, replica_groups=mesh['section'=2,'expert'=16,'dp'=4] {'expert'}, dimensions={1}, use_global_device_ids=true | all-gather | bytes 139264 | tf_op jit(solution)/shard_map/all_gather | solution.py:57
  129.5 14.9 %collective-permute-done.2 = bf16[1,1,192,4096]{3,2,1,0:T(8,128)(2,1)} collective-permute-done((bf16[1,1,192,4096]{3,2,1,0:T(8,128)(2,1)}, bf16[1,1,192,4096]{3,2,1,0:T(8,128)(2,1)}, u32[]{:S(2)}, u32[]{:S(2)}) %collective-permute-start.2) | collective-permute-done | bytes 1572896 | tf_op jit(solution)/shard_map/ppermute | solution.py:45
  144.4 2.8 constant_dynamic-update-slice_fusion.7
  152.4 2.7 constant_dynamic-update-slice_fusion.3
  155.1 2.7 constant_dynamic-update-slice_fusion.2
  160.5 63.3 %all-gather.6.cloned.1.call-done = bf16[1,1,2,4096,768]{4,3,2,1,0:T(8,128)(2,1)} async-done(((bf16[1,1,2,1024,768]{4,3,2,1,0:T(8,128)(2,1)}), bf16[1,1,2,4096,768]{4,3,2,1,0:T(8,128)(2,1)}) %all-gather.6.cloned.1.call-update) | async-done | bytes 12582928 | tf_op jit(solution)/shard_map/all_gather | solution.py:42
  223.7 11.0 %fusion.5 = f32[1024,768]{1,0:T(8,128)S(1)} fusion(bf16[1024,4096]{1,0:T(8,128)(2,1)} %all-gather.4.cloned.1.call-done, bf16[1,1,2,4096,768]{4,3,2,1,0:T(8,128)(2,1)} %all-gather.6.cloned.1.call-done), kind=kOutput, calls=%fused_computation.9 | convolution fusion | flops 6442450944 | bytes 17825792 | tf_op jit(solution)/shard_map/dot_general | solution.py:65
  234.9 7.0 %multiply_convert_fusion.3 = bf16[1024,768]{1,0:T(8,128)(2,1)S(1)} fusion(f32[1024,768]{1,0:T(8,128)S(1)} %fusion.5, bf16[1024,4096]{1,0:T(8,128)(2,1)S(1)} %copy-done.10, bf16[1,1,2,4096,768]{4,3,2,1,0:T(8,128)(2,1)S(1)} %copy-done.9), kind=kOutput, calls=%fused_computation.13 | convolution fusion | flops 6447169536 | bytes 19398656 | tf_op jit(solution)/shard_map/dot_general | solution.py:64
  241.9 11.8 %multiply_convert_fusion.1 = bf16[1024,4096]{1,0:T(8,128)(2,1)} fusion(f32[1024]{0:T(1024)S(1)} %bitcast.45, bf16[1024,768]{1,0:T(8,128)(2,1)S(1)} %multiply_convert_fusion.3, bf16[1,1,1536,4096]{3,2,1,0:T(8,128)(2,1)} %constant_dynamic-update-slice_fusion, s32[]{:T(128)S(6)} %select_n.59), kind=kOutput, calls=%fused_computation.1 | convolution fusion | flops 6450839552 | bytes 16257028 | tf_op jit(solution)/shard_map/dot_general | solution.py:67
  253.8 12.0 %collective-permute-done.6 = bf16[1,1,192,4096]{3,2,1,0:T(8,128)(2,1)} collective-permute-done((bf16[1,1,192,4096]{3,2,1,0:T(8,128)(2,1)}, bf16[1,1,192,4096]{3,2,1,0:T(8,128)(2,1)}, u32[]{:S(2)}, u32[]{:S(2)}) %collective-permute-start.6) | collective-permute-done | bytes 1572896 | tf_op jit(solution)/shard_map/ppermute | solution.py:10
  265.9 102.5 %reduce-scatter.3.cloned.1.call-done = bf16[64,4096]{1,0:T(8,128)(2,1)} async-done(((bf16[1024,4096]{1,0:T(8,128)(2,1)}), bf16[64,4096]{1,0:T(8,128)(2,1)}) %reduce-scatter.3.cloned.1.call-update) | async-done | bytes 524304 | tf_op jit(solution)/shard_map/reduce_scatter | solution.py:71
  372.0 10.2 %collective-permute-done.7 = bf16[64,4096]{1,0:T(8,128)(2,1)S(1)} collective-permute-done((bf16[64,4096]{1,0:T(8,128)(2,1)S(1)}, bf16[64,4096]{1,0:T(8,128)(2,1)S(1)}, u32[]{:S(2)}, u32[]{:S(2)}) %collective-permute-start.7) | collective-permute-done | bytes 524320 | tf_op jit(solution)/shard_map/ppermute | solution.py:16
  384.8 72.7 %all-gather.8.cloned.1.call-done = bf16[1024,4096]{1,0:T(8,128)(2,1)} async-done(((bf16[64,4096]{1,0:T(8,128)(2,1)}), bf16[1024,4096]{1,0:T(8,128)(2,1)}) %all-gather.8.cloned.1.call-update) | async-done | bytes 8388624 | tf_op jit(solution)/shard_map/all_gather | solution.py:63
  457.5 11.0 %fusion.4 = f32[1024,768]{1,0:T(8,128)S(1)} fusion(bf16[1024,4096]{1,0:T(8,128)(2,1)} %all-gather.8.cloned.1.call-done, bf16[1,1,2,4096,768]{4,3,2,1,0:T(8,128)(2,1)} %all-gather.6.cloned.1.call-done), kind=kOutput, calls=%fused_computation.8 | convolution fusion | flops 6442450944 | bytes 17825792 | tf_op jit(solution)/shard_map/dot_general | solution.py:65
  468.5 9.8 %multiply_convert_fusion.2 = bf16[1024,768]{1,0:T(8,128)(2,1)S(1)} fusion(f32[1024,768]{1,0:T(8,128)S(1)} %fusion.4, bf16[1024,4096]{1,0:T(8,128)(2,1)S(1)} %copy-done.11, bf16[1,1,2,4096,768]{4,3,2,1,0:T(8,128)(2,1)} %all-gather.6.cloned.1.call-done), kind=kOutput, calls=%fused_computation.12 | convolution fusion | flops 6447169536 | bytes 19398656 | tf_op jit(solution)/shard_map/dot_general | solution.py:64
  478.3 11.9 %multiply_convert_fusion = bf16[1024,4096]{1,0:T(8,128)(2,1)} fusion(f32[1024]{0:T(1024)S(1)} %bitcast.46, bf16[1024,768]{1,0:T(8,128)(2,1)S(1)} %multiply_convert_fusion.2, bf16[1,1,1536,4096]{3,2,1,0:T(8,128)(2,1)} %constant_dynamic-update-slice_fusion, s32[]{:T(128)S(6)} %select_n.59), kind=kOutput, calls=%fused_computation | convolution fusion | flops 6450839552 | bytes 16257028 | tf_op jit(solution)/shard_map/dot_general | solution.py:67
  491.4 4.8 broadcast_select_fusion
  496.3 3.5 broadcast_select_fusion.3
  499.8 5.0 broadcast_select_fusion.1
  504.7 85.8 %reduce-scatter.5.cloned.1.call-done = bf16[64,4096]{1,0:T(8,128)(2,1)} async-done(((bf16[1024,4096]{1,0:T(8,128)(2,1)}), bf16[64,4096]{1,0:T(8,128)(2,1)}) %reduce-scatter.5.cloned.1.call-update) | async-done | bytes 524304 | tf_op jit(solution)/shard_map/reduce_scatter | solution.py:71
  (70 shorter events, 28.3 us)
Async XLA Ops:
  7.2 4.9 copy-start
  7.2 86.5 %copy-start.7 = (f32[1,2,64,8]{2,3,1,0:T(8,128)S(1)}, f32[1,2,64,8]{2,3,1,0:T(8,128)}, u32[]{:S(2)}) copy-start(f32[1,2,64,8]{2,3,1,0:T(8,128)} %param.18) | copy-start | bytes 12292
  7.2 86.5 %copy-start.8 = (s32[1,2,64,8]{2,3,1,0:T(8,128)S(1)}, s32[1,2,64,8]{2,3,1,0:T(8,128)}, u32[]{:S(2)}) copy-start(s32[1,2,64,8]{2,3,1,0:T(8,128)} %param.17) | copy-start | bytes 12292
  7.2 153.3 %all-gather.4.cloned.1.call-start = ((), (), s32[]{:S(2)}) async-start(), calls=%async_computation.2 | async-start | bytes 8912896 | tf_op jit(solution)/shard_map/all_gather | solution.py:63
  11.2 212.5 %all-gather.6.cloned.1.call-start = ((), (), s32[]{:S(2)}) async-start(), calls=%async_computation.3 | async-start | bytes 15728640 | tf_op jit(solution)/shard_map/all_gather | solution.py:42
  12.0 356.4 %reduce-scatter.3.cloned.1.call-start = ((), (), s32[]{:S(2)}) async-start(), calls=%async_computation.4 | async-start | bytes 8912896 | tf_op jit(solution)/shard_map/reduce_scatter | solution.py:71
  12.0 37.6 %collective-permute-start = (bf16[1,1,192,4096]{3,2,1,0:T(8,128)(2,1)S(1)}, bf16[1,1,192,4096]{3,2,1,0:T(8,128)(2,1)S(1)}, u32[]{:S(2)}, u32[]{:S(2)}) collective-permute-start(bf16[1,1,192,4096]{3,2,1,0:T(8,128)(2,1)S(1)} %copy-done), channel_id=1, source_target_pairs={{0,1},{1,2},{2,3},{3,0},{4,5},{5,6},{6,7},{7,4},{8,9},{9,10},{10,1... | collective-permute-start | bytes 4718600 | tf_op jit(solution)/shard_map/ppermute | solution.py:45
  49.6 36.7 %collective-permute-start.1 = (bf16[1,1,192,4096]{3,2,1,0:T(8,128)(2,1)S(1)}, bf16[1,1,192,4096]{3,2,1,0:T(8,128)(2,1)}, u32[]{:S(2)}, u32[]{:S(2)}) collective-permute-start(bf16[1,1,192,4096]{3,2,1,0:T(8,128)(2,1)S(1)} %collective-permute-done), channel_id=1, source_target_pairs={{0,1},{1,2},{2,3},{3,0},{4,5},{5,6},{6,7},{7,4},{8,9},{9,10},{10,1... | collective-permute-start | bytes 4718600 | tf_op jit(solution)/shard_map/ppermute | solution.py:45
  86.3 58.0 %collective-permute-start.2 = (bf16[1,1,192,4096]{3,2,1,0:T(8,128)(2,1)}, bf16[1,1,192,4096]{3,2,1,0:T(8,128)(2,1)}, u32[]{:S(2)}, u32[]{:S(2)}) collective-permute-start(bf16[1,1,192,4096]{3,2,1,0:T(8,128)(2,1)} %collective-permute-done.1), channel_id=1, source_target_pairs={{0,1},{1,2},{2,3},{3,0},{4,5},{5,6},{6,7},{7,4},{8,9},{9,10},{10,1... | collective-permute-start | bytes 4718600 | tf_op jit(solution)/shard_map/ppermute | solution.py:45
  86.3 179.4 %collective-permute-start.3 = (bf16[1,1,2,1024,768]{4,3,2,1,0:T(8,128)(2,1)}, bf16[1,1,2,1024,768]{4,3,2,1,0:T(8,128)(2,1)}, u32[]{:S(2)}, u32[]{:S(2)}) collective-permute-start(bf16[1,1,2,1024,768]{4,3,2,1,0:T(8,128)(2,1)} %param.13), channel_id=1, source_target_pairs={{0,32},{4,36},{8,40},{12,44},{16,48},{20,52},{24,56},{28,60},{32,0... | collective-permute-start | bytes 9437192 | tf_op jit(solution)/shard_map/ppermute | solution.py:10
  90.1 163.7 %collective-permute-start.4 = (bf16[1,1,192,4096]{3,2,1,0:T(8,128)(2,1)S(1)}, bf16[1,1,192,4096]{3,2,1,0:T(8,128)(2,1)}, u32[]{:S(2)}, u32[]{:S(2)}) collective-permute-start(bf16[1,1,192,4096]{3,2,1,0:T(8,128)(2,1)S(1)} %copy-done), channel_id=1, source_target_pairs={{0,32},{4,36},{8,40},{12,44},{16,48},{20,52},{24,56},{28,60},{32,0... | collective-permute-start | bytes 4718600 | tf_op jit(solution)/shard_map/ppermute | solution.py:10
  90.2 163.6 %collective-permute-start.5 = (bf16[1,1,192,4096]{3,2,1,0:T(8,128)(2,1)}, bf16[1,1,192,4096]{3,2,1,0:T(8,128)(2,1)}, u32[]{:S(2)}, u32[]{:S(2)}) collective-permute-start(bf16[1,1,192,4096]{3,2,1,0:T(8,128)(2,1)} %param.15), channel_id=1, source_target_pairs={{0,32},{4,36},{8,40},{12,44},{16,48},{20,52},{24,56},{28,60},{32,0... | collective-permute-start | bytes 4718600 | tf_op jit(solution)/shard_map/ppermute | solution.py:10
  93.6 172.1 %collective-permute-start.6 = (bf16[1,1,192,4096]{3,2,1,0:T(8,128)(2,1)}, bf16[1,1,192,4096]{3,2,1,0:T(8,128)(2,1)}, u32[]{:S(2)}, u32[]{:S(2)}) collective-permute-start(bf16[1,1,192,4096]{3,2,1,0:T(8,128)(2,1)} %param.16), channel_id=1, source_target_pairs={{0,32},{4,36},{8,40},{12,44},{16,48},{20,52},{24,56},{28,60},{32,0... | collective-permute-start | bytes 4718600 | tf_op jit(solution)/shard_map/ppermute | solution.py:10
  223.7 11.0 %copy-start.9 = (bf16[1,1,2,4096,768]{4,3,2,1,0:T(8,128)(2,1)S(1)}, bf16[1,1,2,4096,768]{4,3,2,1,0:T(8,128)(2,1)}, u32[]{:S(2)}) copy-start(bf16[1,1,2,4096,768]{4,3,2,1,0:T(8,128)(2,1)} %all-gather.6.cloned.1.call-done) | copy-start | bytes 37748740
  223.7 11.2 %copy-start.10 = (bf16[1024,4096]{1,0:T(8,128)(2,1)S(1)}, bf16[1024,4096]{1,0:T(8,128)(2,1)}, u32[]{:S(2)}) copy-start(bf16[1024,4096]{1,0:T(8,128)(2,1)} %all-gather.4.cloned.1.call-done) | copy-start | bytes 25165828
  253.8 114.6 %copy-start.2 = (bf16[64,4096]{1,0:T(8,128)(2,1)S(1)}, bf16[64,4096]{1,0:T(8,128)(2,1)}, u32[]{:S(2)}) copy-start(bf16[64,4096]{1,0:T(8,128)(2,1)} %copy-done.1) | copy-start | bytes 1572868
  253.8 129.7 %copy-start.6 = (f32[1,4096]{1,0:T(1,128)S(1)}, f32[1,4096]{1,0:T(1,128)}, u32[]{:S(2)}) copy-start(f32[1,4096]{1,0:T(1,128)} %param.12) | copy-start | bytes 49156
  253.8 130.8 %copy-start.3 = (f32[1,1024]{0,1:T(8,128)S(1)}, f32[1,1024]{0,1:T(8,128)}, u32[]{:S(2)}) copy-start(f32[1,1024]{0,1:T(8,128)} %get-tuple-element.20) | copy-start | bytes 12292
  265.8 191.7 %all-gather.8.cloned.1.call-start = ((), (), s32[]{:S(2)}) async-start(), calls=%async_computation.5 | async-start | bytes 8912896 | tf_op jit(solution)/shard_map/all_gather | solution.py:63
  369.5 12.7 %collective-permute-start.7 = (bf16[64,4096]{1,0:T(8,128)(2,1)S(1)}, bf16[64,4096]{1,0:T(8,128)(2,1)S(1)}, u32[]{:S(2)}, u32[]{:S(2)}) collective-permute-start(bf16[64,4096]{1,0:T(8,128)(2,1)S(1)} %fusion.11), channel_id=1, source_target_pairs={{0,64},{1,65},{2,66},{3,67},{4,68},{5,69},{6,70},{7,71},{8,72},{9,... | collective-permute-start | bytes 1572872 | tf_op jit(solution)/shard_map/ppermute | solution.py:16
  384.6 206.0 %reduce-scatter.5.cloned.1.call-start = ((), (), s32[]{:S(2)}) async-start(), calls=%async_computation.6 | async-start | bytes 8912896 | tf_op jit(solution)/shard_map/reduce_scatter | solution.py:71
  457.5 11.0 %copy-start.11 = (bf16[1024,4096]{1,0:T(8,128)(2,1)S(1)}, bf16[1024,4096]{1,0:T(8,128)(2,1)}, u32[]{:S(2)}) copy-start(bf16[1024,4096]{1,0:T(8,128)(2,1)} %all-gather.8.cloned.1.call-done) | copy-start | bytes 25165828
  491.4 8.4 %copy-start.4 = (bf16[1,1,192,4096]{3,2,1,0:T(8,128)(2,1)S(1)}, bf16[1,1,192,4096]{3,2,1,0:T(8,128)(2,1)}, u32[]{:S(2)}) copy-start(bf16[1,1,192,4096]{3,2,1,0:T(8,128)(2,1)} %param.16) | copy-start | bytes 4718596
  491.4 8.4 %copy-start.5 = (bf16[1,1,192,4096]{3,2,1,0:T(8,128)(2,1)S(1)}, bf16[1,1,192,4096]{3,2,1,0:T(8,128)(2,1)}, u32[]{:S(2)}) copy-start(bf16[1,1,192,4096]{3,2,1,0:T(8,128)(2,1)} %param.15) | copy-start | bytes 4718596
  (2 other events, 1.5 us)
Sparse Core Ops, SparseCore 0:
  11.3 75.5 all-gather.3
  88.6 135.0 all-gather.5
  265.9 102.3 reduce-scatter.2
  384.7 72.7 all-gather.7
  490.3 100.1 reduce-scatter.4
